TPU v7x, 128 devices: a whole 4x4x4 slice. The times are simulated.
128 devices in a mesh: slab: 16 (over x_hi, z, core), col: 8 (over x_lo, y).
Axes of the slice: x: 4 (x_hi: 2, x_lo: 2; x = x_hi * 2 + x_lo), y: 4, z: 4, core: 2. Of those that a mesh axis runs over, the one named last changes fastest.
Arguments:
- sensitivity: bfloat16 [3, 512, 65536], P(None, 'col', 'slab'), may hold values from -0.03125 to 0.03125
- residual_force: bfloat16 [3, 65536], P(None, 'slab'), may hold values from -6 to 6
- moments: float32 [6, 64, 1024], P(None, 'slab'), as said below
- zone_label: int32 [64, 1024], P('slab'), may hold values from 0 to 511, as said below
- misfit: float32 [64, 1024], P('slab'), may hold values from 0.1 to 10
Outputs:
- hessian: float32 [512, 512], P('col', 'slab')
- gradient: float32 [512], replicated
- zone_misfit: float32 [512], replicated
Inputs may be any that keep to these rules, and one draw needn't show every extreme that they name: zone_label is the box of a 8 x 8 x 8 partition of the specimen that holds the element, the in-plane box borders displaced by at most one element; every zone occurs. `moments`: each element's moment matrix is symmetric with positive diagonal, and each diagonal entry exceeds the sum of the magnitudes of the others in its row.
All inputs are finite; a program needn't handle non-finite values.
Results may differ from a plain program's by a relative error of at most 0.0003.
Values may be sent and summed in bfloat16 or wider, within the bound.
A program may use at most 128 MiB of HBM per device.

v0:
```python
import jax
import jax.numpy as jnp
from jax import lax
from jax.sharding import PartitionSpec as P

GX = 64
GY = 16
third = 1.0 / 3.0
sixth = 1.0 / 6.0


def shifted(value, axis, by):
    count = lax.axis_size(axis)
    pairs = [(i, i + by) for i in range(count) if 0 <= i + by < count]
    return lax.ppermute(value, axis, pairs)


def mix_pair(first, second):
    return (third * first + sixth * second, sixth * first + third * second)


def shift_ahead(field, step, keep):
    moved = jnp.concatenate([field[..., step:], jnp.zeros_like(field[..., :step])], axis=-1)
    if keep is None:
        return moved
    return jnp.where(keep, moved, 0.0)


def shift_behind(field, step, keep):
    moved = jnp.concatenate([jnp.zeros_like(field[..., :step]), field[..., :-step]], axis=-1)
    if keep is None:
        return moved
    return jnp.where(keep, moved, 0.0)


def apply_moments(moments, field):
    comps = [moments[k][None, :] for k in range(6)]
    first, second, last = (field[0], field[1], field[2])
    out_x = comps[0] * first + comps[3] * second + comps[4] * last
    out_y = comps[3] * first + comps[1] * second + comps[5] * last
    out_z = comps[4] * first + comps[5] * second + comps[2] * last
    return jnp.stack([out_x, out_y, out_z])


def element_layer(lower, upper, moments):
    plane = lower.shape[-1]
    pos_y = jnp.arange(plane, dtype=jnp.int32) % GY
    not_last = pos_y != GY - 1
    not_first = pos_y != 0
    mixed_z = mix_pair(lower, upper)
    results = []
    for side_z in range(2):
        field = mixed_z[side_z]
        mixed_x = mix_pair(field, shift_ahead(field, GY, None))
        values = []
        for side_x in range(2):
            layer = mixed_x[side_x]
            mixed_y = mix_pair(layer, shift_ahead(layer, 1, not_last))
            values.append([apply_moments(moments, mixed_y[side_y]) for side_y in range(2)])
        total = values[0][0]
        total = total + shift_behind(values[1][0], GY, None)
        total = total + shift_behind(values[0][1], 1, not_first)
        total = total + shift_behind(shift_behind(values[1][1], 1, not_first), GY, None)
        results.append(total)
    return (results[0], results[1])


def on_device(sensitivity, residual_force, moments, zone_label, misfit):
    cols = sensitivity.shape[1]
    layers = moments.shape[1]
    plane_size = GX * GY
    n_slab = lax.axis_size("slab")
    n_col = lax.axis_size("col")
    width = cols * n_col
    field = sensitivity.reshape(3, cols, layers, plane_size)
    above = shifted(sensitivity[:, :, :plane_size], "slab", -1)
    levels = []
    carry = None
    first_lower = None
    for level in range(layers):
        lower = field[:, :, level].astype(jnp.float32)
        if level + 1 < layers:
            upper = field[:, :, level + 1].astype(jnp.float32)
        else:
            upper = above.astype(jnp.float32)
        to_lower, to_upper = element_layer(lower, upper, moments[:, level])
        if level == 0:
            first_lower = to_lower
        else:
            levels.append((carry + to_lower).astype(jnp.bfloat16))
        carry = to_upper
    from_below = shifted(carry.astype(jnp.bfloat16), "slab", 1).astype(carry.dtype)
    levels.insert(0, (from_below + first_lower).astype(jnp.bfloat16))
    image = jnp.stack(levels, axis=2).reshape(3, cols, layers * plane_size)
    panel_rows = lax.dot_general(
        image,
        lax.all_gather(sensitivity, "col", axis=1, tiled=True),
        (((0, 2), (0, 2)), ((), ())),
        preferred_element_type=jnp.float32,
    )
    hessian = lax.psum_scatter(panel_rows, "slab", scatter_dimension=1, tiled=True)
    grad_part = lax.dot_general(
        residual_force,
        sensitivity,
        (((0, 1), (0, 2)), ((), ())),
        preferred_element_type=jnp.float32,
    )
    grad_full = lax.dynamic_update_slice_in_dim(
        jnp.zeros((width,), jnp.float32), grad_part, lax.axis_index("col") * cols, 0
    )
    elements = layers * plane_size
    share = elements // n_col
    offset = lax.axis_index("col") * share
    zone_part = lax.dynamic_slice_in_dim(zone_label.reshape(elements), offset, share, 0)
    misfit_part = lax.dynamic_slice_in_dim(misfit.reshape(elements), offset, share, 0)
    onehot = (zone_part[:, None] == jnp.arange(width, dtype=jnp.int32)[None, :]).astype(jnp.float32)
    zone_part_sum = jnp.dot(misfit_part, onehot, precision=lax.Precision.HIGHEST)
    gradient, zone_sums = lax.psum((grad_full, zone_part_sum), ("slab", "col"))
    zone_misfit = zone_sums * (width / (elements * n_slab))
    return (hessian, gradient, zone_misfit)


def solution(mesh):
    in_specs = (
        P(None, "col", "slab"),
        P(None, "slab"),
        P(None, "slab", None),
        P("slab", None),
        P("slab", None),
    )
    out_specs = (P("col", "slab"), P(), P())
    return jax.shard_map(
        on_device, mesh=mesh, in_specs=in_specs, out_specs=out_specs, check_vma=False
    )
```

profile of v0, /device:TPU:0, one launch (start us, length us, event | category | flops | bytes accessed | tf_op | source)
XLA Modules:
  0.0 330.2 jit_solution(12702796365399645540)
XLA Ops:
  9.3 1.3 collective-permute-start
  10.6 1.2 reshape.1815
  11.8 3.2 fusion.94
  19.5 1.4 fusion.96
  22.2 1.3 multiply_add_fusion.41
  24.0 1.4 slice.1015
  25.4 2.3 slice.999
  30.2 161.3 %all-reduce.56 = (f32[512]{0:T(512)}, f32[512]{0:T(512)}) all-reduce(f32[512]{0:T(512)S(1)} %dynamic_update_slice.3, f32[512]{0:T(512)S(1)} %bitcast.370), channel_id=1, replica_groups=mesh['slab'=16,'col'=8] {'slab','col'}, use_global_device_ids=true, to_apply=%region_1.2 | all-reduce | flops 1024 | bytes 8192 | tf_op jit(solution)/shard_map/psum | solution.py:118
  192.8 1.5 fusion.3
  194.6 1.2 fusion.5
  196.2 2.6 multiply_add_fusion.45
  204.6 1.2 slice.953
  215.7 1.2 slice.1036
  216.9 5.2 %multiply_add_fusion.42 = (f32[3,64,1024]{2,1,0:T(8,128)}, f32[3,64,1024]{2,1,0:T(8,128)}, f32[3,64,1024]{2,1,0:T(8,128)S(1)}, f32[3,64,1024]{2,1,0:T(8,128)S(1)...) fusion(f32[3,64,1024]{2,1,0:T(8,128)S(1)} %get-tuple-element.43, ...), kind=kLoop, calls=%fused_computation.212 | loop fusion | flops 8257536 | bytes 18870784 | tf_op jit(solution)/shard_map/add | solution.py:19
  222.1 2.1 multiply_add_fusion.122
  225.2 5.7 %multiply_add_fusion.46 = (f32[3,64,1024]{2,1,0:T(8,128)}, f32[3,64,1024]{2,1,0:T(8,128)}, f32[3,64,1024]{2,1,0:T(8,128)}, f32[3,64,1024]{2,1,0:T(8,128)S(1)}, f...) fusion(f32[3,64,1024]{2,1,0:T(8,128)S(1)} %get-tuple-element.44, ...), kind=kLoop, calls=%fused_computation.217 | loop fusion | flops 8257536 | bytes 18870784 | tf_op jit(solution)/shard_map/add | solution.py:19
  231.0 1.3 multiply_add_fusion.98
  236.0 1.5 fusion.76
  238.3 1.8 collective-permute-start.1
  245.9 1.4 fusion.87
  247.3 1.3 fusion.86
  248.6 1.3 fusion.85
  251.0 7.1 %convolution_bitcast_fusion = f32[64,512]{0,1:T(8,128)} fusion(bf16[3,64,4096]{2,1,0:T(8,128)(2,1)S(1)} %bitcast.171, bf16[3,512,4096]{2,1,0:T(8,128)(2,1)} %all-gather.2.cloned.1.call-done), kind=kOutput, calls=%fused_computation.1 | convolution fusion | flops 805306368 | bytes 14286848 | tf_op jit(solution)/shard_map/dot_general | solution.py:95
  258.7 64.7 %reduce-scatter.2.cloned.1.call-done = f32[64,32]{0,1:T(8,128)} async-done(((f32[64,512]{0,1:T(8,128)}), f32[64,32]{0,1:T(8,128)}) %reduce-scatter.2.cloned.1.call-update) | async-done | bytes 8208 | tf_op jit(solution)/shard_map/reduce_scatter | solution.py:101
  (184 shorter events, 40.9 us)
Async XLA Ops:
  7.2 243.8 %all-gather.2.cloned.1.call-start = ((), (), s32[]{:S(2)}) async-start(), calls=%async_computation.1 | async-start | bytes 14155776 | tf_op jit(solution)/shard_map/all_gather | solution.py:97
  7.9 315.5 %reduce-scatter.2.cloned.1.call-start = ((), (), s32[]{:S(2)}) async-start(), calls=%async_computation.2 | async-start | bytes 278528 | tf_op jit(solution)/shard_map/reduce_scatter | solution.py:101
  9.3 183.5 %collective-permute-start = (bf16[3,64,1024]{2,1,0:T(8,128)(2,1)}, bf16[3,64,1024]{2,1,0:T(8,128)(2,1)}, u32[]{:S(2)}, u32[]{:S(2)}) collective-permute-start(bf16[3,64,1024]{2,1,0:T(8,128)(2,1)} %slice.768), channel_id=1, source_target_pairs={{8,0},{16,8},{24,16},{32,24},{40,32},{48,40},{56,48},{64,56},{72,6... | collective-permute-start | bytes 1179656 | tf_op jit(solution)/shard_map/ppermute | solution.py:15
  15.9 2.4 copy-start.47
  15.9 2.4 copy-start.48
  15.9 2.6 copy-start.51
  17.2 3.8 %copy-start.19 = (bf16[3,64,1,1024]{3,2,1,0:T(2,128)(2,1)S(1)}, bf16[3,64,1,1024]{3,2,1,0:T(2,128)(2,1)}, u32[]{:S(2)}) copy-start(bf16[3,64,1,1024]{3,2,1,0:T(2,128)(2,1)} %get-tuple-element.57) | copy-start | bytes 1179652
  19.1 3.1 copy-start.4
  19.1 3.1 copy-start.18
  27.7 164.5 %copy-start.45 = (f32[6,4,1024]{2,1,0:T(4,128)S(1)}, f32[6,4,1024]{2,1,0:T(4,128)}, u32[]{:S(2)}) copy-start(f32[6,4,1024]{2,1,0:T(4,128)} %param.7) | copy-start | bytes 294916
  216.9 5.2 %copy-start.25 = (f32[1,1,1024]{2,1,0:T(1,128)S(1)}, f32[1,1,1024]{2,1,0:T(1,128)}, u32[]{:S(2)}) copy-start(f32[1,1,1024]{2,1,0:T(1,128)} %get-tuple-element.188) | copy-start | bytes 12292
  216.9 5.2 %copy-start.26 = (f32[1,1,1024]{2,1,0:T(1,128)S(1)}, f32[1,1,1024]{2,1,0:T(1,128)}, u32[]{:S(2)}) copy-start(f32[1,1,1024]{2,1,0:T(1,128)} %get-tuple-element.189) | copy-start | bytes 12292
  225.2 5.7 %copy-start.29 = (f32[1,1,1024]{2,1,0:T(1,128)S(1)}, f32[1,1,1024]{2,1,0:T(1,128)}, u32[]{:S(2)}) copy-start(f32[1,1,1024]{2,1,0:T(1,128)} %get-tuple-element.179) | copy-start | bytes 12292
  225.2 5.7 %copy-start.30 = (f32[1,1,1024]{2,1,0:T(1,128)S(1)}, f32[1,1,1024]{2,1,0:T(1,128)}, u32[]{:S(2)}) copy-start(f32[1,1,1024]{2,1,0:T(1,128)} %get-tuple-element.180) | copy-start | bytes 12292
  225.2 5.7 %copy-start.31 = (f32[1,1,1024]{2,1,0:T(1,128)S(1)}, f32[1,1,1024]{2,1,0:T(1,128)}, u32[]{:S(2)}) copy-start(f32[1,1,1024]{2,1,0:T(1,128)} %get-tuple-element.181) | copy-start | bytes 12292
  225.2 5.7 %copy-start.32 = (f32[1,1,1024]{2,1,0:T(1,128)S(1)}, f32[1,1,1024]{2,1,0:T(1,128)}, u32[]{:S(2)}) copy-start(f32[1,1,1024]{2,1,0:T(1,128)} %get-tuple-element.182) | copy-start | bytes 12292
  225.2 5.7 %copy-start.33 = (f32[1,1,1024]{2,1,0:T(1,128)S(1)}, f32[1,1,1024]{2,1,0:T(1,128)}, u32[]{:S(2)}) copy-start(f32[1,1,1024]{2,1,0:T(1,128)} %get-tuple-element.183) | copy-start | bytes 12292
  225.2 5.7 %copy-start.34 = (f32[1,1,1024]{2,1,0:T(1,128)S(1)}, f32[1,1,1024]{2,1,0:T(1,128)}, u32[]{:S(2)}) copy-start(f32[1,1,1024]{2,1,0:T(1,128)} %get-tuple-element.184) | copy-start | bytes 12292
  237.6 2.6 copy-start.13
  237.6 2.6 copy-start.14
  237.6 2.6 copy-start.15
  237.6 2.6 copy-start.16
  238.3 11.5 %collective-permute-start.1 = (bf16[3,64,1024]{2,1,0:T(8,128)(2,1)S(1)}, bf16[3,64,1024]{2,1,0:T(8,128)(2,1)S(1)}, u32[]{:S(2)}, u32[]{:S(2)}) collective-permute-start(bf16[3,64,1024]{2,1,0:T(8,128)(2,1)S(1)} %fusion.81), channel_id=1, source_target_pairs={{0,8},{8,16},{16,24},{24,32},{32,40},{40,48},{48,56},{56,64},{64,7... | collective-permute-start | bytes 1179656 | tf_op jit(solution)/shard_map/ppermute | solution.py:15
  251.0 7.1 %copy-start.50 = (f32[512]{0:T(512)S(1)}, f32[512]{0:T(512)}, u32[]{:S(2)}) copy-start(f32[512]{0:T(512)} %get-tuple-element.4) | copy-start | bytes 6148
  (32 other events, 43.4 us)
Sparse Core Ops, SparseCore 0:
  9.6 134.1 all-gather.1
  258.2 65.1 reduce-scatter.1
where the time goes:
time: 331 us; the launch traced here: 330 us
  blocking collectives  161 us (49%)
  waiting for transfers between devices  65.4 us (20%)
  other arithmetic  38.8 us (12%)
  local copies, waits for them, and re-layouts  38.6 us (12%)
  between operations  14.8 us (4%)
  matrix products  8.09 us (2%)
    psum x1, blocking collectives, on_device(): gradient, zone_sums = lax.psum((grad_full, zone_part_sum), ('slab', 'col'))  161 us
    reduce_scatter x1, waiting for transfers between devices, on_device(): lax.psum_scatter(panel_rows, 'slab', scatter_dimension=1, tiled=True)  64.7 us
    slice x24, local copies, waits for them, and re-layouts, shift_ahead(): field[..., step:]  24.9 us
    add x11, other arithmetic, mix_pair(): return (third * first + sixth * second, sixth * first + third * second)  21 us
    add x32, other arithmetic, apply_moments(): out_x = comps[0] * first + comps[3] * second + comps[4] * last  8.5 us
    dot_general x1, matrix products, on_device(): lax.dot_general(image, lax.all_gather(sensitivity, 'col', axis=1, tiled=T...  7.08 us
  transfers between devices with their start and end apart: 4, of which 1 were waited for; matrix products, arithmetic and copies ran while one was open for 22% of the time, Pallas kernels for 0%

commit v1 on v0

--- a/solution.py
+++ b/solution.py
@@ -115,7 +115,7 @@
     misfit_part = lax.dynamic_slice_in_dim(misfit.reshape(elements), offset, share, 0)
     onehot = (zone_part[:, None] == jnp.arange(width, dtype=jnp.int32)[None, :]).astype(jnp.float32)
     zone_part_sum = jnp.dot(misfit_part, onehot, precision=lax.Precision.HIGHEST)
-    gradient, zone_sums = lax.psum((grad_full, zone_part_sum), ("slab", "col"))
+    gradient, zone_sums = lax.psum(lax.psum((grad_full, zone_part_sum), "slab"), "col")
     zone_misfit = zone_sums * (width / (elements * n_slab))
     return (hessian, gradient, zone_misfit)
 

time: 331 us -> 231 us (0.70)
  blocking collectives: 161 us -> 63.2 us
    psum x1 -> x2, blocking collectives: 161 us -> 63.2 us  [the longest x1 43.2 us: on_device(): lax.psum((grad_full, zone_part_sum), 'slab')]
  transfers between devices with their start and end apart: 4 -> 4, of which waited for: 1 -> 1; matrix products, arithmetic and copies ran while one was open for 22% -> 32% of each run, Pallas kernels for 0% -> 0%
where the time goes in v1:
time: 231 us; the launch traced here: 230 us
  waiting for transfers between devices  63.6 us (28%)
  blocking collectives  63.2 us (27%)
  other arithmetic  39 us (17%)
  local copies, waits for them, and re-layouts  38.7 us (17%)
  between operations  14.8 us (6%)
  matrix products  8.1 us (4%)
  starting transfers between devices  2.8 us (1%)
    reduce_scatter x1, waiting for transfers between devices, on_device(): lax.psum_scatter(panel_rows, 'slab', scatter_dimension=1, tiled=True)  62.9 us
    psum x1, blocking collectives, on_device(): lax.psum((grad_full, zone_part_sum), 'slab')  43.2 us
    slice x24, local copies, waits for them, and re-layouts, shift_ahead(): field[..., step:]  25 us
    add x11, other arithmetic, mix_pair(): return (third * first + sixth * second, sixth * first + third * second)  21.2 us
    psum x1, blocking collectives, on_device(): lax.psum(lax.psum((grad_full, zone_part_sum), 'slab'), 'col')  20 us
    add x32, other arithmetic, apply_moments(): out_x = comps[0] * first + comps[3] * second + comps[4] * last  8.53 us
    dot_general x1, matrix products, on_device(): lax.dot_general(image, lax.all_gather(sensitivity, 'col', axis=1, tiled=T...  7.08 us
    unnamed x106, local copies, waits for them, and re-layouts  6.02 us
  transfers between devices with their start and end apart: 4, of which 1 were waited for; matrix products, arithmetic and copies ran while one was open for 32% of the time, Pallas kernels for 0%

profile of v1, /device:TPU:0, one launch (start us, length us, event | category | flops | bytes accessed | tf_op | source)
XLA Modules:
  0.0 230.2 jit_solution(7889365594550435397)
XLA Ops:
  9.3 1.3 collective-permute-start
  11.8 3.2 %fusion.94 = (bf16[3,64,1,1024]{3,2,1,0:T(2,128)(2,1)}, bf16[3,64,1,1024]{3,2,1,0:T(2,128)(2,1)S(1)}, bf16[3,64,1,1024]{3,2,1,0:T(2,128)(2,1)}, bf16[3,64,1,1024]{3,2,1,0:T(2,128)(2,1)S(1)}) fusion(bf16[3,64,4,1024]{3,2,1,0:T(4,128)(2,1)S(1)} %reshape.1815), kind=kLoop, calls=%fused_computation.332 | loop fusion | bytes 3145728 | tf_op jit(solution)/shard_map/slice | solution.py:83
  19.6 1.4 fusion.96
  22.2 1.3 multiply_add_fusion.41
  24.1 1.4 slice.1015
  25.5 2.3 %slice.999 = f32[3,64,1008]{2,1,0:T(8,128)} slice(f32[3,64,1024]{2,1,0:T(8,128)} %get-tuple-element.11), slice={[0:3], [0:64], [16:1024]} | slice | bytes 1548288 | tf_op jit(solution)/shard_map/slice | solution.py:23
  30.3 43.2 %all-reduce.56 = (f32[512]{0:T(512)S(1)}, f32[512]{0:T(512)S(1)}) all-reduce(f32[512]{0:T(512)S(1)} %dynamic_update_slice.3, f32[512]{0:T(512)S(1)} %bitcast.370), channel_id=1, replica_groups=mesh['slab'=16,'col'=8] {'slab'}, use_global_device_ids=true, to_apply=%region_1.2 | all-reduce | flops 1024 | bytes 8192 | tf_op jit(solution)/shard_map/psum | solution.py:118
  73.5 20.0 %all-reduce.57 = (f32[512]{0:T(512)}, f32[512]{0:T(512)}) all-reduce(f32[512]{0:T(512)S(1)} %get-tuple-element.3, f32[512]{0:T(512)S(1)} %get-tuple-element.4), channel_id=1, replica_groups=mesh['slab'=16,'col'=8] {'col'}, use_global_device_ids=true, to_apply=%region_2.3 | all-reduce | flops 1024 | bytes 8192 | tf_op jit(solution)/shard_map/psum | solution.py:118
  94.7 1.5 fusion.3
  96.6 1.2 fusion.5
  98.1 2.6 %multiply_add_fusion.45 = (f32[3,64,1024]{2,1,0:T(8,128)S(1)}, f32[3,64,1024]{2,1,0:T(8,128)S(1)}, f32[3,64,1024]{2,1,0:T(8,128)S(1)}, f32[3,64,1024]{2,1,0:T(8,...) fusion(f32[3,64,1008]{2,1,0:T(8,128)S(1)} %slice.948, ...), kind=kLoop, calls=%fused_computation.216 | loop fusion | flops 8847360 | bytes 13713408 | tf_op jit(solution)/shard_map/add | solution.py:19
  106.6 1.2 slice.953
  114.2 1.2 slice.1016
  118.9 5.3 %multiply_add_fusion.42 = (f32[3,64,1024]{2,1,0:T(8,128)}, f32[3,64,1024]{2,1,0:T(8,128)}, f32[3,64,1024]{2,1,0:T(8,128)S(1)}, f32[3,64,1024]{2,1,0:T(8,128)S(1)...) fusion(f32[3,64,1024]{2,1,0:T(8,128)S(1)} %get-tuple-element.45, ...), kind=kLoop, calls=%fused_computation.212 | loop fusion | flops 8257536 | bytes 18870784 | tf_op jit(solution)/shard_map/add | solution.py:19
  124.2 2.2 multiply_add_fusion.122
  127.3 5.8 %multiply_add_fusion.46 = (f32[3,64,1024]{2,1,0:T(8,128)}, f32[3,64,1024]{2,1,0:T(8,128)}, f32[3,64,1024]{2,1,0:T(8,128)}, f32[3,64,1024]{2,1,0:T(8,128)S(1)}, f...) fusion(f32[3,64,1024]{2,1,0:T(8,128)S(1)} %get-tuple-element.46, ...), kind=kLoop, calls=%fused_computation.217 | loop fusion | flops 8257536 | bytes 18870784 | tf_op jit(solution)/shard_map/add | solution.py:19
  133.2 1.3 multiply_add_fusion.98
  138.2 1.5 fusion.76
  140.5 1.4 collective-permute-start.1
  147.7 1.4 fusion.87
  149.1 1.3 fusion.86
  150.4 1.3 fusion.85
  152.8 7.1 %convolution_bitcast_fusion = f32[64,512]{0,1:T(8,128)} fusion(bf16[3,64,4096]{2,1,0:T(8,128)(2,1)S(1)} %bitcast.171, bf16[3,512,4096]{2,1,0:T(8,128)(2,1)} %all-gather.2.cloned.1.call-done), kind=kOutput, calls=%fused_computation.1 | convolution fusion | flops 805306368 | bytes 14286848 | tf_op jit(solution)/shard_map/dot_general | solution.py:95
  160.5 62.9 %reduce-scatter.2.cloned.1.call-done = f32[64,32]{0,1:T(8,128)} async-done(((f32[64,512]{0,1:T(8,128)}), f32[64,32]{0,1:T(8,128)}) %reduce-scatter.2.cloned.1.call-update) | async-done | bytes 8208 | tf_op jit(solution)/shard_map/reduce_scatter | solution.py:101
  (185 shorter events, 42.2 us)
Async XLA Ops:
  7.2 145.6 %all-gather.2.cloned.1.call-start = ((), (), s32[]{:S(2)}) async-start(), calls=%async_computation.1 | async-start | bytes 14155776 | tf_op jit(solution)/shard_map/all_gather | solution.py:97
  7.9 215.5 %reduce-scatter.2.cloned.1.call-start = ((), (), s32[]{:S(2)}) async-start(), calls=%async_computation.2 | async-start | bytes 278528 | tf_op jit(solution)/shard_map/reduce_scatter | solution.py:101
  9.3 85.4 %collective-permute-start = (bf16[3,64,1024]{2,1,0:T(8,128)(2,1)}, bf16[3,64,1024]{2,1,0:T(8,128)(2,1)}, u32[]{:S(2)}, u32[]{:S(2)}) collective-permute-start(bf16[3,64,1024]{2,1,0:T(8,128)(2,1)} %slice.768), channel_id=1, source_target_pairs={{8,0},{16,8},{24,16},{32,24},{40,32},{48,40},{56,48},{64,56},{72,6... | collective-permute-start | bytes 1179656 | tf_op jit(solution)/shard_map/ppermute | solution.py:15
  15.9 2.5 %copy-start.47 = (f32[4,1024]{1,0:T(4,128)S(1)}, f32[4,1024]{1,0:T(4,128)}, u32[]{:S(2)}) copy-start(f32[4,1024]{1,0:T(4,128)} %param.9) | copy-start | bytes 49156
  15.9 2.5 %copy-start.48 = (s32[4,1024]{1,0:T(4,128)S(1)}, s32[4,1024]{1,0:T(4,128)}, u32[]{:S(2)}) copy-start(s32[4,1024]{1,0:T(4,128)} %param.8) | copy-start | bytes 49156
  16.0 2.6 %copy-start.51 = (bf16[3,4096]{1,0:T(4,128)(2,1)S(1)}, bf16[3,4096]{1,0:T(4,128)(2,1)}, u32[]{:S(2)}) copy-start(bf16[3,4096]{1,0:T(4,128)(2,1)} %param.6) | copy-start | bytes 73732
  17.2 3.8 %copy-start.19 = (bf16[3,64,1,1024]{3,2,1,0:T(2,128)(2,1)S(1)}, bf16[3,64,1,1024]{3,2,1,0:T(2,128)(2,1)}, u32[]{:S(2)}) copy-start(bf16[3,64,1,1024]{3,2,1,0:T(2,128)(2,1)} %get-tuple-element.59) | copy-start | bytes 1179652
  19.1 3.1 %copy-start.4 = (f32[3,64,1024]{2,1,0:T(8,128)S(1)}, f32[3,64,1024]{2,1,0:T(8,128)}, u32[]{:S(2)}) copy-start(f32[3,64,1024]{2,1,0:T(8,128)} %copy-done.3) | copy-start | bytes 2359300
  19.1 3.1 %copy-start.18 = (f32[3,64,1008]{2,1,0:T(8,128)S(1)}, f32[3,64,1008]{2,1,0:T(8,128)}, u32[]{:S(2)}) copy-start(f32[3,64,1008]{2,1,0:T(8,128)} %slice.966) | copy-start | bytes 2322436
  27.8 66.3 %copy-start.45 = (f32[6,4,1024]{2,1,0:T(4,128)S(1)}, f32[6,4,1024]{2,1,0:T(4,128)}, u32[]{:S(2)}) copy-start(f32[6,4,1024]{2,1,0:T(4,128)} %param.7) | copy-start | bytes 294916
  116.5 2.3 %copy-start.49 = (pred[1024]{0:T(1024)(128)(4,1)S(1)}, pred[1024]{0:T(1024)(128)(4,1)}, u32[]{:S(2)}) copy-start(pred[1024]{0:T(1024)(128)(4,1)} %fusion.92) | copy-start | bytes 3076
  118.9 5.3 %copy-start.25 = (f32[1,1,1024]{2,1,0:T(1,128)S(1)}, f32[1,1,1024]{2,1,0:T(1,128)}, u32[]{:S(2)}) copy-start(f32[1,1,1024]{2,1,0:T(1,128)} %get-tuple-element.190) | copy-start | bytes 12292
  118.9 5.3 %copy-start.26 = (f32[1,1,1024]{2,1,0:T(1,128)S(1)}, f32[1,1,1024]{2,1,0:T(1,128)}, u32[]{:S(2)}) copy-start(f32[1,1,1024]{2,1,0:T(1,128)} %get-tuple-element.191) | copy-start | bytes 12292
  127.3 5.8 %copy-start.29 = (f32[1,1,1024]{2,1,0:T(1,128)S(1)}, f32[1,1,1024]{2,1,0:T(1,128)}, u32[]{:S(2)}) copy-start(f32[1,1,1024]{2,1,0:T(1,128)} %get-tuple-element.181) | copy-start | bytes 12292
  127.3 5.8 %copy-start.30 = (f32[1,1,1024]{2,1,0:T(1,128)S(1)}, f32[1,1,1024]{2,1,0:T(1,128)}, u32[]{:S(2)}) copy-start(f32[1,1,1024]{2,1,0:T(1,128)} %get-tuple-element.182) | copy-start | bytes 12292
  127.3 5.8 %copy-start.31 = (f32[1,1,1024]{2,1,0:T(1,128)S(1)}, f32[1,1,1024]{2,1,0:T(1,128)}, u32[]{:S(2)}) copy-start(f32[1,1,1024]{2,1,0:T(1,128)} %get-tuple-element.183) | copy-start | bytes 12292
  127.3 5.8 %copy-start.32 = (f32[1,1,1024]{2,1,0:T(1,128)S(1)}, f32[1,1,1024]{2,1,0:T(1,128)}, u32[]{:S(2)}) copy-start(f32[1,1,1024]{2,1,0:T(1,128)} %get-tuple-element.184) | copy-start | bytes 12292
  127.3 5.8 %copy-start.33 = (f32[1,1,1024]{2,1,0:T(1,128)S(1)}, f32[1,1,1024]{2,1,0:T(1,128)}, u32[]{:S(2)}) copy-start(f32[1,1,1024]{2,1,0:T(1,128)} %get-tuple-element.185) | copy-start | bytes 12292
  127.3 5.8 %copy-start.34 = (f32[1,1,1024]{2,1,0:T(1,128)S(1)}, f32[1,1,1024]{2,1,0:T(1,128)}, u32[]{:S(2)}) copy-start(f32[1,1,1024]{2,1,0:T(1,128)} %get-tuple-element.186) | copy-start | bytes 12292
  139.8 2.2 copy-start.13
  139.8 2.2 copy-start.14
  139.8 2.2 copy-start.15
  140.5 11.1 %collective-permute-start.1 = (bf16[3,64,1024]{2,1,0:T(8,128)(2,1)S(1)}, bf16[3,64,1024]{2,1,0:T(8,128)(2,1)S(1)}, u32[]{:S(2)}, u32[]{:S(2)}) collective-permute-start(bf16[3,64,1024]{2,1,0:T(8,128)(2,1)S(1)} %fusion.81), channel_id=1, source_target_pairs={{0,8},{8,16},{16,24},{24,32},{32,40},{40,48},{48,56},{56,64},{64,7... | collective-permute-start | bytes 1179656 | tf_op jit(solution)/shard_map/ppermute | solution.py:15
  152.8 7.1 %copy-start.50 = (f32[512]{0:T(512)S(1)}, f32[512]{0:T(512)}, u32[]{:S(2)}) copy-start(f32[512]{0:T(512)} %get-tuple-element.6) | copy-start | bytes 6148
  (32 other events, 43.3 us)
Sparse Core Ops, SparseCore 0:
  9.6 134.3 all-gather.1
  160.0 63.3 reduce-scatter.1
